TPU v7x, 256 devices: a whole 4x4x8 slice. The times are simulated.
256 devices in a mesh: seq: 64 (over z, x, core), head: 4 (over y).
Axes of the slice: x: 4, y: 4, z: 8, core: 2. Of those that a mesh axis runs over, the one named last changes fastest.
Arguments:
- queries: bfloat16 [32768, 4096], P('seq', 'head'), may hold values from -6 to 6
- keys: bfloat16 [32768, 4096], P('seq', 'head'), may hold values from -6 to 6
- values: bfloat16 [32768, 4096], P('seq', 'head'), may hold values from -6 to 6
- med_weight: float32 [2, 32, 4], P(None, 'head'), may hold values from -3 to 3
- coarse_weight: float32 [2, 32, 64], P(None, 'head'), may hold values from -0.75 to 0.75
- out_weight: bfloat16 [4096, 4096], P('head'), may hold values from -0.09375 to 0.09375
Outputs:
- mixed: bfloat16 [32768, 4096], P('seq', 'head')
All inputs are finite; a program needn't handle non-finite values.
Results may differ from a plain program's by a relative error of at most 0.013.
Values may be sent and summed in bfloat16 or wider, within the bound.
No kernel may reach another device: no remote copies, remote signals or barrier semaphores. Data moves between devices by JAX's collectives and lax.ppermute only.
A program may use at most 128 MiB of HBM per device.

v0:
```python
import functools
import math

import jax
import jax.numpy as jnp
from jax import lax
from jax.experimental import pallas as pl
from jax.experimental.pallas import tpu as pltpu
from jax.sharding import PartitionSpec as P

HEAD_DIM = 128
WIN = 512
MED = 4
COARSE = 64
CHIPS_X = 4
PLANE = 2 * CHIPS_X
PLANES = 8
NEG = -1e30
EXP2_SCALE = math.log2(math.e) / math.sqrt(HEAD_DIM)
F32 = jnp.float32
BF16 = jnp.bfloat16
HBM = pl.BlockSpec(memory_space=pltpu.HBM)
VMEM = pl.BlockSpec(memory_space=pltpu.VMEM)
SMEM = pl.BlockSpec(memory_space=pltpu.SMEM)


def in_hbm(x):
    return pltpu.with_memory_space_constraint(x, pltpu.HBM)


def mm(a, b):
    return lax.dot_general(a, b, (((1,), (0,)), ((), ())), preferred_element_type=F32)


def mm_t(a, b):
    return lax.dot_general(a, b, (((1,), (1,)), ((), ())), preferred_element_type=F32)


def head_cols(h):
    return pl.ds(h * HEAD_DIM, HEAD_DIM)


def fetch_heads(pairs, sems, heads):
    copies = []
    for h in range(heads):
        copies.append(
            [
                pltpu.make_async_copy(
                    src.at[:, head_cols(h)], dst.at[:, head_cols(h)], sems.at[t, h]
                )
                for t, (src, dst) in enumerate(pairs)
            ]
        )
        for copy in copies[h]:
            copy.start()
    return copies


def pool_kernel(
    heads,
    k_hbm, v_hbm, mw_ref, cw_hbm,
    med_ref, coarse_ref,
    k_ref, v_ref, cw_ref, rows_ref, sems, w_sem,
):
    w_copy = pltpu.make_async_copy(cw_hbm, cw_ref, w_sem.at[0])
    w_copy.start()
    copies = fetch_heads(((k_hbm, k_ref), (v_hbm, v_ref)), sems, heads)
    rows = k_ref.shape[0]
    n_med, n_coarse = rows // MED, rows // COARSE
    lane = lax.broadcasted_iota(jnp.int32, (heads, rows), 1)
    for slot, (ref, ratio) in enumerate(((mw_ref, MED), (cw_ref, COARSE))):
        at = lane % ratio
        if slot:
            w_copy.wait()
        for t in range(2):
            w = ref[t]
            spread = jnp.zeros((heads, rows), F32)
            for r in range(ratio):
                spread = jnp.where(at == r, w[:, r : r + 1], spread)
            high = spread.astype(BF16).astype(F32)
            rows_ref[slot, 0, t] = high
            rows_ref[slot, 1, t] = spread - high

    def on(n, ratio):
        source = lax.broadcasted_iota(jnp.int32, (n, rows), 1)
        return source // ratio == lax.broadcasted_iota(jnp.int32, (n, rows), 0)

    med_on, coarse_on = on(n_med, MED), on(n_coarse, COARSE)
    for h in range(heads):
        for copy in copies[h]:
            copy.wait()
        for t, ref in enumerate((k_ref, v_ref)):
            row = pl.ds(h, 1)
            left = []
            for part in range(2):
                left.append(jnp.where(med_on, rows_ref[0, part, t, row, :], 0.0))
                left.append(jnp.where(coarse_on, rows_ref[1, part, t, row, :], 0.0))
            r = mm(jnp.concatenate(left, axis=0).astype(BF16), ref[:, head_cols(h)])
            r = r[: n_med + n_coarse] + r[n_med + n_coarse :]
            med_ref[t, :, head_cols(h)] = r[:n_med].astype(BF16)
            coarse_ref[:, head_cols(t * heads + h)] = r[n_med:].astype(BF16)


def pool(keys, values, med_weight, coarse_weight):
    rows, width = keys.shape
    heads = width // HEAD_DIM
    return pl.pallas_call(
        functools.partial(pool_kernel, heads),
        out_shape=(jax.ShapeDtypeStruct((2, rows // MED, width), BF16),
            jax.ShapeDtypeStruct((rows // COARSE, 2 * width), BF16),
        ),
        in_specs=[HBM, HBM, VMEM, HBM],
        out_specs=(VMEM, VMEM),
        scratch_shapes=[
            pltpu.VMEM((rows, width), BF16),
            pltpu.VMEM((rows, width), BF16),
            pltpu.VMEM(coarse_weight.shape, F32),
            pltpu.VMEM((2, 2, 2, heads, rows), F32),
            pltpu.SemaphoreType.DMA((2, heads)),
            pltpu.SemaphoreType.DMA((1,)),
        ],
        compiler_params=pltpu.CompilerParams(vmem_limit_bytes=12 << 20),
        cost_estimate=pl.CostEstimate(
            flops=4 * 136 * rows * 2 * width, bytes_accessed=3 << 20, transcendentals=0
        ),
        name="pool",
    )(
        in_hbm(keys),
        in_hbm(values),
        med_weight,
        in_hbm(coarse_weight),
    )


def weigh(scores, peak, values):
    p = jnp.exp2((scores - peak) * EXP2_SCALE).astype(BF16)
    return mm(p, jnp.concatenate([values, jnp.ones_like(values)], axis=1))


def near_kernel(
    tile, heads,
    pos_ref, q_hbm, k_hbm, v_hbm, ek_hbm, ev_hbm,
    acc_ref, peak_ref,
    q_ref, k_ref, v_ref, sems,
):
    rows, n_edge = q_ref.shape[0], ek_hbm.shape[0]
    own, edge = pl.ds(n_edge, rows), pl.ds(0, n_edge)
    copies = fetch_heads(
        (
            (q_hbm, q_ref),
            (k_hbm, k_ref.at[own, :]),
            (v_hbm, v_ref.at[own, :]),
            (ek_hbm, k_ref.at[edge, :]),
            (ev_hbm, v_ref.at[edge, :]),
        ),
        sems,
        heads,
    )
    has_edge = pos_ref[0] >= 1
    on_diag = lax.broadcasted_iota(jnp.int32, (tile, tile), 1) <= lax.broadcasted_iota(
        jnp.int32, (tile, tile), 0
    )
    for h in range(heads):
        for copy in copies[h]:
            copy.wait()
        c = head_cols(h)
        for i in range(rows // tile):
            at, n = pl.ds(i * tile, tile), n_edge + i * tile
            s = mm_t(q_ref[at, c], k_ref[: n + tile, c])
            parts = [jnp.where(has_edge, s[:, :n_edge], NEG)]
            if i:
                parts.append(s[:, n_edge:n])
            parts.append(jnp.where(on_diag, s[:, n:], NEG))
            s = jnp.concatenate(parts, axis=1)
            peak = jnp.max(s, axis=1, keepdims=True)
            acc_ref[at, pl.ds(2 * h * HEAD_DIM, 2 * HEAD_DIM)] = weigh(
                s, peak, v_ref[: n + tile, c]
            )
            peak_ref[at, c] = jnp.broadcast_to(peak, (tile, HEAD_DIM))


def near(position, queries, keys, values, edge_keys, edge_values):
    rows, width = queries.shape
    heads = width // HEAD_DIM
    n_keys = edge_keys.shape[0] + rows
    return pl.pallas_call(
        functools.partial(near_kernel, 256, heads),
        out_shape=(
            jax.ShapeDtypeStruct((rows, 2 * width), F32),
            jax.ShapeDtypeStruct((rows, width), F32),
        ),
        in_specs=[SMEM] + [HBM] * 5,
        out_specs=(VMEM, VMEM),
        scratch_shapes=[
            pltpu.VMEM((rows, width), BF16),
            pltpu.VMEM((n_keys, width), BF16),
            pltpu.VMEM((n_keys, width), BF16),
            pltpu.SemaphoreType.DMA((5, heads)),
        ],
        compiler_params=pltpu.CompilerParams(vmem_limit_bytes=24 << 20),
        cost_estimate=pl.CostEstimate(
            flops=rows * n_keys * width, bytes_accessed=1 << 20, transcendentals=0
        ),
        name="near",
    )(position, *[in_hbm(x) for x in (queries, keys, values, edge_keys)], edge_values)


def far_kernel(
    tile, heads, members, per_coarse,
    pos_ref, head_ref, q_hbm, m2, m3, m4, mine, other, acc_hbm, peak_hbm, w_hbm,
    att_ref, left_ref, right_ref,
    q_ref, k_ref, v_ref, acc_ref, peak_ref, w_ref, sems, w_sem,
):
    rows, width = att_ref.shape
    n_med, n_coarse = m2.shape[1], mine.shape[0]
    groups = heads // 2

    def whole(src, dst, g, per):
        cols = pl.ds(g * per, per)
        return src.at[:, cols], dst.at[:, cols]

    def part(src, dst, g, to, shift=0):
        size = src.shape[0]
        return (
            src.at[:, pl.ds(shift + g * 2 * HEAD_DIM, 2 * HEAD_DIM)],
            dst.at[pl.ds(to, size), pl.ds(g * 2 * HEAD_DIM, 2 * HEAD_DIM)],
        )

    def group_copies(g):
        pairs = [whole(q_hbm, q_ref, g, 2 * HEAD_DIM)]
        to = 0
        for m in (m2, m3, m4):
            pairs += [part(m.at[0], k_ref, g, to), part(m.at[1], v_ref, g, to)]
            to += n_med
        for c in (mine, other):
            pairs += [part(c, k_ref, g, to), part(c, v_ref, g, to, width)]
            to += n_coarse
        pairs.append(whole(acc_hbm, acc_ref, g, 4 * HEAD_DIM))
        pairs.append(whole(peak_hbm, peak_ref, g, 2 * HEAD_DIM))
        return [
            pltpu.make_async_copy(src, dst, sems.at[t, g]) for t, (src, dst) in enumerate(pairs)
        ]

    copies = [group_copies(g) for g in range(groups)]
    block = lax.rem(head_ref[0] + 2, members)
    cols = pl.ds(pl.multiple_of(block * width, width), width)
    w_copy = pltpu.make_async_copy(w_hbm.at[:, cols], w_ref, w_sem.at[0])
    for g in range(2):
        for copy in copies[g]:
            copy.start()
    w_copy.start()
    pos = pos_ref[0]
    j = lax.broadcasted_iota(jnp.int32, (1, n_coarse), 1) // per_coarse
    group = j // (2 * CHIPS_X)
    step = jnp.where(group == 3, -1, group)
    z = (pos // PLANE + step + 4 * (j % 2)) & (PLANES - 1)
    x = (pos % PLANE // 2 - j // 2 % CHIPS_X) & (CHIPS_X - 1)
    bias = [
        jnp.where(pos >= d, jnp.zeros((1, n_med), F32), jnp.full((1, n_med), NEG, F32))
        for d in (2, 3, 4)
    ]
    for core in (pos % 2, 1 - pos % 2):
        bias.append(jnp.where(z * PLANE + x * 2 + core < pos, 0.0, NEG))
    bias = jnp.concatenate(bias, axis=1)
    for h in range(heads):
        if h % 2 == 0:
            for copy in copies[h // 2]:
                copy.wait()
            if h // 2 + 2 < groups:
                for copy in copies[h // 2 + 2]:
                    copy.start()
        c = head_cols(h)
        for i in range(rows // tile):
            at = pl.ds(i * tile, tile)
            s = mm_t(q_ref[at, c], k_ref[:, c]) + bias
            near_peak = peak_ref[at, c]
            peak = jnp.maximum(near_peak, jnp.max(s, axis=1, keepdims=True))
            shrink = jnp.exp2((near_peak - peak) * EXP2_SCALE)
            got = weigh(s, peak[:, :1], v_ref[:, c])
            near_acc = acc_ref[at, head_cols(2 * h)]
            near_total = acc_ref[at, head_cols(2 * h + 1)]
            att_ref[at, c] = (
                (near_acc * shrink + got[:, :HEAD_DIM])
                / (near_total * shrink + got[:, HEAD_DIM:])
            ).astype(BF16)
    w_copy.wait()
    middle = width // 2
    left_ref[...] = mm(att_ref[...], w_ref[:, :middle]).astype(BF16)
    right_ref[...] = mm(att_ref[...], w_ref[:, middle:]).astype(BF16)


def far(position, head, queries, meds, coarse, acc, peak, weight):
    rows, width = queries.shape
    heads = width // HEAD_DIM
    members = weight.shape[1] // width
    n_keys = 3 * meds[0].shape[1] + 2 * coarse[0].shape[0]
    half = jax.ShapeDtypeStruct((rows, width // 2), BF16)
    return pl.pallas_call(
        functools.partial(far_kernel, 256, heads, members, rows // COARSE),
        out_shape=(jax.ShapeDtypeStruct((rows, width), BF16), half, half),
        in_specs=[SMEM, SMEM] + [HBM] * 9,
        out_specs=(VMEM, VMEM, VMEM),
        scratch_shapes=[
            pltpu.VMEM((rows, width), BF16),
            pltpu.VMEM((n_keys, width), BF16),
            pltpu.VMEM((n_keys, width), BF16),
            pltpu.VMEM((rows, 2 * width), F32),
            pltpu.VMEM((rows, width), F32),
            pltpu.VMEM((width, width), BF16),
            pltpu.SemaphoreType.DMA((13, heads // 2)),
            pltpu.SemaphoreType.DMA((1,)),
        ],
        compiler_params=pltpu.CompilerParams(vmem_limit_bytes=36 << 20),
        cost_estimate=pl.CostEstimate(
            flops=8 * rows * n_keys * width, bytes_accessed=2 << 20, transcendentals=0
        ),
        name="far",
    )(
        position,
        head,
        in_hbm(queries),
        in_hbm(meds[0]),
        meds[1],
        in_hbm(meds[2]),
        *coarse,
        in_hbm(acc),
        in_hbm(peak),
        in_hbm(weight),
    )


def project_kernel(members, order, head_ref, a_ref, w_hbm, *refs):
    outs, (w_ref, sems) = refs[: len(order)], refs[len(order) :]
    width = outs[0].shape[1]
    copies = []
    for i, k in enumerate(order):
        block = lax.rem(head_ref[0] + k, members)
        cols = pl.ds(pl.multiple_of(block * width, width), width)
        copies.append(pltpu.make_async_copy(w_hbm.at[:, cols], w_ref.at[i], sems.at[i]))
        copies[i].start()
    for i, out in enumerate(outs):
        copies[i].wait()
        out[...] = mm(a_ref[...], w_ref[i]).astype(BF16)


def project(head, attention, weight, members, order):
    rows, depth = attention.shape
    width = weight.shape[1] // members
    return pl.pallas_call(
        functools.partial(project_kernel, members, order),
        out_shape=[jax.ShapeDtypeStruct((rows, width), BF16)] * len(order),
        in_specs=[SMEM, VMEM, HBM],
        out_specs=[VMEM] * len(order),
        scratch_shapes=[
            pltpu.VMEM((len(order), depth, width), BF16),
            pltpu.SemaphoreType.DMA((len(order),)),
        ],
        compiler_params=pltpu.CompilerParams(vmem_limit_bytes=24 << 20),
        cost_estimate=pl.CostEstimate(
            flops=2 * rows * depth * width * len(order),
            bytes_accessed=6 << 20,
            transcendentals=0,
        ),
        name="project",
    )(head, attention, in_hbm(weight))


def shifted(block, axis, distance):
    devices = range(lax.axis_size(axis))
    return lax.ppermute(
        block, axis, [(i - distance, i) for i in devices if i - distance in devices]
    )


def body(queries, keys, values, med_weight, coarse_weight, out_weight):
    n_seq = lax.axis_size("seq")
    members = lax.axis_size("head")
    position = lax.axis_index("seq")
    pos = position.astype(jnp.int32).reshape(1)
    head = lax.axis_index("head").astype(jnp.int32).reshape(1)
    core0 = (position & 1) == 0
    swap = [(i, i ^ 1) for i in range(n_seq)]

    def place(z, x, core):
        return z * PLANE + x * 2 + core

    def move(block, dz, dx):
        route = [
            (place(z, x, c), place((z + dz) % PLANES, (x + dx) % CHIPS_X, c))
            for z in range(PLANES)
            for x in range(CHIPS_X)
            for c in range(2)
        ]
        return lax.ppermute(block, "seq", route)

    edge_keys = shifted(keys, "seq", 1)
    med, coarse = pool(keys, values, med_weight, coarse_weight)
    quad = jnp.concatenate([coarse, move(coarse, 4, 0)], 0)
    ring = jnp.concatenate([quad] + [move(quad, 0, d) for d in range(1, CHIPS_X)], 0)

    edge_keys, values, ring, med = lax.optimization_barrier((edge_keys, values, ring, med))
    edge_values = shifted(values, "seq", 1)
    rings = [move(ring, d, 0) for d in (-1, -2, 1)]
    med2 = shifted(med, "seq", 2)
    med4 = shifted(med, "seq", 4)
    acc, peak = near(pos, queries, keys, values, edge_keys, edge_values)
    rings, med2, med4, acc, peak = lax.optimization_barrier((rings, med2, med4, acc, peak))
    mine = jnp.concatenate([ring] + rings, 0)
    other = lax.ppermute(mine, "seq", swap)
    med3 = lax.ppermute(jnp.where(core0, med2, med4), "seq", swap)

    def send(block, distance):
        return lax.ppermute(
            block, "head", [(i, (i + distance) % members) for i in range(members)]
        )

    attention, left, right = far(
        pos, head, queries, (med2, med3, med4), (mine, other), acc, peak, out_weight
    )
    left, right = send(left, 1), send(right, -1)
    ahead, behind, own = project(head, attention, out_weight, members, (1, members - 1, 0))
    middle = left.shape[1]

    def plus(a, b):
        return (a.astype(F32) + b.astype(F32)).astype(BF16)

    ahead = jnp.concatenate([plus(ahead[:, :middle], left), ahead[:, middle:]], 1)
    behind = jnp.concatenate([behind[:, :middle], plus(behind[:, middle:], right)], 1)
    ahead, behind = send(ahead, 1), send(behind, -1)
    return (own.astype(F32) + ahead.astype(F32) + behind.astype(F32)).astype(BF16)


def solution(mesh):
    placed = (
        P("seq", "head"),
        P("seq", "head"),
        P("seq", "head"),
        P(None, "head", None),
        P(None, "head", None),
        P("head", None),
    )
    return jax.shard_map(
        body, mesh=mesh, in_specs=placed, out_specs=P("seq", "head"), check_vma=False
    )
```

profile of v0, /device:TPU:96, one launch (start us, length us, event | category | flops | bytes accessed | tf_op | source)
XLA Modules:
  0.0 137.7 jit_solution(11253950527712662756)
XLA Ops:
  0.0 1.9 %collective-permute-start = (bf16[512,1024]{1,0:T(8,128)(2,1)}, bf16[512,1024]{1,0:T(8,128)(2,1)S(1)}, u32[]{:S(2)}, u32[]{:S(2)}) collective-permute-start(bf16[512,1024]{1,0:T(8,128)(2,1)} %k_hbm.3), channel_id=1, source_target_pairs={{0,4},{4,8},{8,12},{12,16},{16,20},{20,24},{24,28},{28,32},{32,36}... | collective-permute-start | bytes 3145736 | tf_op jit(solution)/shard_map/ppermute | solution.py:370
  2.7 4.5 %pool.1 = (bf16[2,128,1024]{2,1,0:T(8,128)(2,1)S(1)}, bf16[8,2048]{1,0:T(8,128)(2,1)S(1)}) custom-call(bf16[512,1024]{1,0:T(8,128)(2,1)} %k_hbm.3, bf16[512,1024]{1,0:T(8,128)(2,1)} %v_hbm.2, f32[2,8,4]{2,1,0:T(8,128)S(1)} %copy.7.mw_ref, f32[2,8,64]{2,1,0:T(8,128)} %cw_hbm.1), custom_call_target="tpu_custom_call" | custom-call | flops 570425344 | bytes 3145728 | tf_op jit(solution)/shard_map/pool/pallas_call | solution.py:107
  7.2 4.6 %collective-permute-start.1 = (bf16[8,2048]{1,0:T(8,128)(2,1)S(1)}, bf16[8,2048]{1,0:T(8,128)(2,1)S(1)}, u32[]{:S(2)}, u32[]{:S(2)}) collective-permute-start(bf16[8,2048]{1,0:T(8,128)(2,1)S(1)} %get-tuple-element.26), channel_id=1, source_target_pairs={{0,128},{4,132},{8,136},{12,140},{16,144},{20,148},{24,152},{28,15... | collective-permute-start | bytes 98312 | tf_op jit(solution)/shard_map/ppermute | solution.py:394
  11.8 3.3 %collective-permute-done.1 = bf16[8,2048]{1,0:T(8,128)(2,1)S(1)} collective-permute-done((bf16[8,2048]{1,0:T(8,128)(2,1)S(1)}, bf16[8,2048]{1,0:T(8,128)(2,1)S(1)}, u32[]{:S(2)}, u32[]{:S(2)}) %collective-permute-start.1) | collective-permute-done | bytes 32800 | tf_op jit(solution)/shard_map/ppermute | solution.py:394
  18.3 1.8 %collective-permute-start.3 = (bf16[16,2048]{1,0:T(8,128)(2,1)S(1)}, bf16[16,2048]{1,0:T(8,128)(2,1)S(1)}, u32[]{:S(2)}, u32[]{:S(2)}) collective-permute-start(bf16[16,2048]{1,0:T(8,128)(2,1)S(1)} %get-tuple-element.47), channel_id=1, source_target_pairs={{0,16},{4,20},{8,24},{12,28},{16,0},{20,4},{24,8},{28,12},{32,48},... | collective-permute-start | bytes 196616 | tf_op jit(solution)/shard_map/ppermute | solution.py:394
  20.6 4.0 %collective-permute-done.3 = bf16[16,2048]{1,0:T(8,128)(2,1)S(1)} collective-permute-done((bf16[16,2048]{1,0:T(8,128)(2,1)S(1)}, bf16[16,2048]{1,0:T(8,128)(2,1)S(1)}, u32[]{:S(2)}, u32[]{:S(2)}) %collective-permute-start.3) | collective-permute-done | bytes 65568 | tf_op jit(solution)/shard_map/ppermute | solution.py:394
  25.5 2.0 %collective-permute-start.10 = (bf16[512,1024]{1,0:T(8,128)(2,1)}, bf16[512,1024]{1,0:T(8,128)(2,1)S(1)}, u32[]{:S(2)}, u32[]{:S(2)}) collective-permute-start(bf16[512,1024]{1,0:T(8,128)(2,1)} %v_hbm.2), channel_id=1, source_target_pairs={{0,4},{4,8},{8,12},{12,16},{16,20},{20,24},{24,28},{28,32},{32,36}... | collective-permute-start | bytes 3145736 | tf_op jit(solution)/shard_map/ppermute | solution.py:370
  27.6 3.8 %collective-permute-start.9 = (bf16[2,128,1024]{2,1,0:T(8,128)(2,1)S(1)}, bf16[2,128,1024]{2,1,0:T(8,128)(2,1)S(1)}, u32[]{:S(2)}, u32[]{:S(2)}) collective-permute-start(bf16[2,128,1024]{2,1,0:T(8,128)(2,1)S(1)} %get-tuple-element.29), channel_id=1, source_target_pairs={{0,16},{4,20},{8,24},{12,28},{16,32},{20,36},{24,40},{28,44},{32,4... | collective-permute-start | bytes 1572872 | tf_op jit(solution)/shard_map/ppermute | solution.py:370
  31.4 2.4 %collective-permute-start.8 = (bf16[2,128,1024]{2,1,0:T(8,128)(2,1)S(1)}, bf16[2,128,1024]{2,1,0:T(8,128)(2,1)}, u32[]{:S(2)}, u32[]{:S(2)}) collective-permute-start(bf16[2,128,1024]{2,1,0:T(8,128)(2,1)S(1)} %get-tuple-element.29), channel_id=1, source_target_pairs={{0,8},{4,12},{8,16},{12,20},{16,24},{20,28},{24,32},{28,36},{32,40... | collective-permute-start | bytes 1572872 | tf_op jit(solution)/shard_map/ppermute | solution.py:370
  33.8 3.2 %collective-permute-start.7 = (bf16[64,2048]{1,0:T(8,128)(2,1)S(1)}, bf16[64,2048]{1,0:T(8,128)(2,1)S(1)}, u32[]{:S(2)}, u32[]{:S(2)}) collective-permute-start(bf16[64,2048]{1,0:T(8,128)(2,1)S(1)} %constant_dynamic-update-slice_fusion.2), channel_id=1, source_target_pairs={{0,32},{4,36},{8,40},{12,44},{16,48},{20,52},{24,56},{28,60},{32,6... | collective-permute-start | bytes 786440 | tf_op jit(solution)/shard_map/ppermute | solution.py:394
  37.0 2.6 %collective-permute-start.6 = (bf16[64,2048]{1,0:T(8,128)(2,1)S(1)}, bf16[64,2048]{1,0:T(8,128)(2,1)S(1)}, u32[]{:S(2)}, u32[]{:S(2)}) collective-permute-start(bf16[64,2048]{1,0:T(8,128)(2,1)S(1)} %constant_dynamic-update-slice_fusion.2), channel_id=1, source_target_pairs={{0,192},{4,196},{8,200},{12,204},{16,208},{20,212},{24,216},{28,22... | collective-permute-start | bytes 786440 | tf_op jit(solution)/shard_map/ppermute | solution.py:394
  39.6 19.9 %collective-permute-done.10.ev_hbm = bf16[512,1024]{1,0:T(8,128)(2,1)S(1)} collective-permute-done((bf16[512,1024]{1,0:T(8,128)(2,1)}, bf16[512,1024]{1,0:T(8,128)(2,1)S(1)}, u32[]{:S(2)}, u32[]{:S(2)}) %collective-permute-start.10) | collective-permute-done | bytes 1048608 | tf_op jit(solution)/shard_map/ppermute | solution.py:370
  59.5 11.1 %near.1 = (f32[512,2048]{1,0:T(8,128)S(1)}, f32[512,1024]{1,0:T(8,128)S(1)}) custom-call(s32[1]{0:T(128)} %bitcast.1.pos_ref, bf16[512,1024]{1,0:T(8,128)(2,1)} %q_hbm.3, bf16[512,1024]{1,0:T(8,128)(2,1)} %k_hbm.3, bf16[512,1024]{1,0:T(8,128)(2,1)} %v_hbm.2, bf16[512,1024]{1,0:T(8,128)(2,1)} %copy-done.3, bf16[512,1024]{1,0:T(8,128)(2,1)S(1)} %collective-permute-done.10.ev_hbm), custom_call_target="tpu_custom_call" | custom-call | flops 536870912 | bytes 1048576 | tf_op jit(solution)/shard_map/near/pallas_call | solution.py:186
  70.6 1.9 %copy-done = f32[512,2048]{1,0:T(8,128)} copy-done((f32[512,2048]{1,0:T(8,128)}, f32[512,2048]{1,0:T(8,128)S(1)}, u32[]{:S(2)}) %copy-start) | copy-done | bytes 4194328
  74.0 2.0 %collective-permute-start.12 = (bf16[256,2048]{1,0:T(8,128)(2,1)S(1)}, bf16[256,2048]{1,0:T(8,128)(2,1)S(1)}, u32[]{:S(2)}, u32[]{:S(2)}) collective-permute-start(bf16[256,2048]{1,0:T(8,128)(2,1)S(1)} %constant_dynamic-update-slice_fusion.7.mine), channel_id=1, source_target_pairs={{0,4},{4,0},{8,12},{12,8},{16,20},{20,16},{24,28},{28,24},{32,36},... | collective-permute-start | bytes 3145736 | tf_op jit(solution)/shard_map/ppermute | solution.py:409
  76.0 1.9 %broadcast_select_fusion = bf16[2,128,1024]{2,1,0:T(8,128)(2,1)} fusion(bf16[2,128,1024]{2,1,0:T(8,128)(2,1)} %collective-permute-done.8.m2, bf16[2,128,1024]{2,1,0:T(8,128)(2,1)S(1)} %collective-permute-done.9.m4, pred[]{:T(512)S(6)} %eq.3), kind=kLoop, calls=%fused_computation.5 | loop fusion | flops 262144 | bytes 1572865 | tf_op jit(solution)/shard_map/jit(_where)/select_n | solution.py:410
  77.9 2.1 %collective-permute-done.11.m3 = bf16[2,128,1024]{2,1,0:T(8,128)(2,1)S(1)} collective-permute-done((bf16[2,128,1024]{2,1,0:T(8,128)(2,1)}, bf16[2,128,1024]{2,1,0:T(8,128)(2,1)S(1)}, u32[]{:S(2)}, u32[]{:S(2)}) %collective-permute-start.11) | collective-permute-done | bytes 524320 | tf_op jit(solution)/shard_map/ppermute | solution.py:410
  80.0 11.7 %far.1 = (bf16[512,1024]{1,0:T(8,128)(2,1)S(1)}, bf16[512,512]{1,0:T(8,128)(2,1)S(1)}, bf16[512,512]{1,0:T(8,128)(2,1)S(1)}) custom-call(s32[1]{0:T(128)} %bitcast.1.pos_ref, s32[1]{0:T(128)} %bitcast.head_ref, bf16[512,1024]{1,0:T(8,128)(2,1)} %q_hbm.3, bf16[2,128,1024]{2,1,0:T(8,128)(2,1)} %collective-permute-done.8.m2, ...), custom_call_target="tpu_custom_call" | custom-call | flops 3758096384 | bytes 2097152 | tf_op jit(solution)/shard_map/far/pallas_call | solution.py:298
  91.7 3.1 %collective-permute-start.15 = (bf16[512,512]{1,0:T(8,128)(2,1)S(1)}, bf16[512,512]{1,0:T(8,128)(2,1)S(1)}, u32[]{:S(2)}, u32[]{:S(2)}) collective-permute-start(bf16[512,512]{1,0:T(8,128)(2,1)S(1)} %get-tuple-element.46), channel_id=1, source_target_pairs={{0,3},{1,0},{2,1},{3,2},{4,7},{5,4},{6,5},{7,6},{8,11},{9,8},{10,9... | collective-permute-start | bytes 1572872 | tf_op jit(solution)/shard_map/ppermute | solution.py:413
  94.8 5.4 %project.1 = (bf16[512,1024]{1,0:T(8,128)(2,1)S(1)}, bf16[512,1024]{1,0:T(8,128)(2,1)S(1)}, bf16[512,1024]{1,0:T(8,128)(2,1)S(1)}) custom-call(s32[1]{0:T(128)} %bitcast.head_ref, bf16[512,1024]{1,0:T(8,128)(2,1)S(1)} %get-tuple-element.41.a_ref, bf16[1024,4096]{1,0:T(8,128)(2,1)} %w_hbm.3), custom_call_target="tpu_custom_call" | custom-call | flops 3221225472 | bytes 6291456 | tf_op jit(solution)/shard_map/project/pallas_call | solution.py:349
  100.3 6.0 %collective-permute-done.15 = bf16[512,512]{1,0:T(8,128)(2,1)S(1)} collective-permute-done((bf16[512,512]{1,0:T(8,128)(2,1)S(1)}, bf16[512,512]{1,0:T(8,128)(2,1)S(1)}, u32[]{:S(2)}, u32[]{:S(2)}) %collective-permute-start.15) | collective-permute-done | bytes 524320 | tf_op jit(solution)/shard_map/ppermute | solution.py:413
  106.6 3.8 %collective-permute-start.16 = (bf16[512,1024]{1,0:T(8,128)(2,1)S(1)}, bf16[512,1024]{1,0:T(8,128)(2,1)S(1)}, u32[]{:S(2)}, u32[]{:S(2)}) collective-permute-start(bf16[512,1024]{1,0:T(8,128)(2,1)S(1)} %pad_maximum_fusion.1), channel_id=1, source_target_pairs={{0,3},{1,0},{2,1},{3,2},{4,7},{5,4},{6,5},{7,6},{8,11},{9,8},{10,9... | collective-permute-start | bytes 3145736 | tf_op jit(solution)/shard_map/ppermute | solution.py:413
  110.8 21.5 %collective-permute-done.16 = bf16[512,1024]{1,0:T(8,128)(2,1)S(1)} collective-permute-done((bf16[512,1024]{1,0:T(8,128)(2,1)S(1)}, bf16[512,1024]{1,0:T(8,128)(2,1)S(1)}, u32[]{:S(2)}, u32[]{:S(2)}) %collective-permute-start.16) | collective-permute-done | bytes 1048608 | tf_op jit(solution)/shard_map/ppermute | solution.py:413
  132.3 3.8 %collective-permute-done.14 = bf16[512,1024]{1,0:T(8,128)(2,1)S(1)} collective-permute-done((bf16[512,1024]{1,0:T(8,128)(2,1)S(1)}, bf16[512,1024]{1,0:T(8,128)(2,1)S(1)}, u32[]{:S(2)}, u32[]{:S(2)}) %collective-permute-start.14) | collective-permute-done | bytes 1048608 | tf_op jit(solution)/shard_map/ppermute | solution.py:413
  (40 shorter events, 9.3 us)
Async XLA Ops:
  0.0 24.6 %collective-permute-start = (bf16[512,1024]{1,0:T(8,128)(2,1)}, bf16[512,1024]{1,0:T(8,128)(2,1)S(1)}, u32[]{:S(2)}, u32[]{:S(2)}) collective-permute-start(bf16[512,1024]{1,0:T(8,128)(2,1)} %k_hbm.3), channel_id=1, source_target_pairs={{0,4},{4,8},{8,12},{12,16},{16,20},{20,24},{24,28},{28,32},{32,36}... | collective-permute-start | bytes 3145736 | tf_op jit(solution)/shard_map/ppermute | solution.py:370
  7.2 7.9 %collective-permute-start.1 = (bf16[8,2048]{1,0:T(8,128)(2,1)S(1)}, bf16[8,2048]{1,0:T(8,128)(2,1)S(1)}, u32[]{:S(2)}, u32[]{:S(2)}) collective-permute-start(bf16[8,2048]{1,0:T(8,128)(2,1)S(1)} %get-tuple-element.26), channel_id=1, source_target_pairs={{0,128},{4,132},{8,136},{12,140},{16,144},{20,148},{24,152},{28,15... | collective-permute-start | bytes 98312 | tf_op jit(solution)/shard_map/ppermute | solution.py:394
  15.1 5.5 %collective-permute-start.2 = (bf16[16,2048]{1,0:T(8,128)(2,1)S(1)}, bf16[16,2048]{1,0:T(8,128)(2,1)S(1)}, u32[]{:S(2)}, u32[]{:S(2)}) collective-permute-start(bf16[16,2048]{1,0:T(8,128)(2,1)S(1)} %get-tuple-element.47), channel_id=1, source_target_pairs={{0,8},{4,12},{8,16},{12,20},{16,24},{20,28},{24,0},{28,4},{32,40},... | collective-permute-start | bytes 196616 | tf_op jit(solution)/shard_map/ppermute | solution.py:394
  16.6 8.0 %collective-permute-start.4 = (bf16[16,2048]{1,0:T(8,128)(2,1)S(1)}, bf16[16,2048]{1,0:T(8,128)(2,1)S(1)}, u32[]{:S(2)}, u32[]{:S(2)}) collective-permute-start(bf16[16,2048]{1,0:T(8,128)(2,1)S(1)} %get-tuple-element.47), channel_id=1, source_target_pairs={{0,24},{4,28},{8,0},{12,4},{16,8},{20,12},{24,16},{28,20},{32,56},... | collective-permute-start | bytes 196616 | tf_op jit(solution)/shard_map/ppermute | solution.py:394
  18.3 6.2 %collective-permute-start.3 = (bf16[16,2048]{1,0:T(8,128)(2,1)S(1)}, bf16[16,2048]{1,0:T(8,128)(2,1)S(1)}, u32[]{:S(2)}, u32[]{:S(2)}) collective-permute-start(bf16[16,2048]{1,0:T(8,128)(2,1)S(1)} %get-tuple-element.47), channel_id=1, source_target_pairs={{0,16},{4,20},{8,24},{12,28},{16,0},{20,4},{24,8},{28,12},{32,48},... | collective-permute-start | bytes 196616 | tf_op jit(solution)/shard_map/ppermute | solution.py:394
  24.6 1.0 copy-start.3
  25.5 33.9 %collective-permute-start.10 = (bf16[512,1024]{1,0:T(8,128)(2,1)}, bf16[512,1024]{1,0:T(8,128)(2,1)S(1)}, u32[]{:S(2)}, u32[]{:S(2)}) collective-permute-start(bf16[512,1024]{1,0:T(8,128)(2,1)} %v_hbm.2), channel_id=1, source_target_pairs={{0,4},{4,8},{8,12},{12,16},{16,20},{20,24},{24,28},{28,32},{32,36}... | collective-permute-start | bytes 3145736 | tf_op jit(solution)/shard_map/ppermute | solution.py:370
  27.6 46.4 %collective-permute-start.9 = (bf16[2,128,1024]{2,1,0:T(8,128)(2,1)S(1)}, bf16[2,128,1024]{2,1,0:T(8,128)(2,1)S(1)}, u32[]{:S(2)}, u32[]{:S(2)}) collective-permute-start(bf16[2,128,1024]{2,1,0:T(8,128)(2,1)S(1)} %get-tuple-element.29), channel_id=1, source_target_pairs={{0,16},{4,20},{8,24},{12,28},{16,32},{20,36},{24,40},{28,44},{32,4... | collective-permute-start | bytes 1572872 | tf_op jit(solution)/shard_map/ppermute | solution.py:370
  31.4 42.5 %collective-permute-start.8 = (bf16[2,128,1024]{2,1,0:T(8,128)(2,1)S(1)}, bf16[2,128,1024]{2,1,0:T(8,128)(2,1)}, u32[]{:S(2)}, u32[]{:S(2)}) collective-permute-start(bf16[2,128,1024]{2,1,0:T(8,128)(2,1)S(1)} %get-tuple-element.29), channel_id=1, source_target_pairs={{0,8},{4,12},{8,16},{12,20},{16,24},{20,28},{24,32},{28,36},{32,40... | collective-permute-start | bytes 1572872 | tf_op jit(solution)/shard_map/ppermute | solution.py:370
  33.8 40.1 %collective-permute-start.7 = (bf16[64,2048]{1,0:T(8,128)(2,1)S(1)}, bf16[64,2048]{1,0:T(8,128)(2,1)S(1)}, u32[]{:S(2)}, u32[]{:S(2)}) collective-permute-start(bf16[64,2048]{1,0:T(8,128)(2,1)S(1)} %constant_dynamic-update-slice_fusion.2), channel_id=1, source_target_pairs={{0,32},{4,36},{8,40},{12,44},{16,48},{20,52},{24,56},{28,60},{32,6... | collective-permute-start | bytes 786440 | tf_op jit(solution)/shard_map/ppermute | solution.py:394
  37.0 36.9 %collective-permute-start.6 = (bf16[64,2048]{1,0:T(8,128)(2,1)S(1)}, bf16[64,2048]{1,0:T(8,128)(2,1)S(1)}, u32[]{:S(2)}, u32[]{:S(2)}) collective-permute-start(bf16[64,2048]{1,0:T(8,128)(2,1)S(1)} %constant_dynamic-update-slice_fusion.2), channel_id=1, source_target_pairs={{0,192},{4,196},{8,200},{12,204},{16,208},{20,212},{24,216},{28,22... | collective-permute-start | bytes 786440 | tf_op jit(solution)/shard_map/ppermute | solution.py:394
  59.5 14.4 %collective-permute-start.5 = (bf16[64,2048]{1,0:T(8,128)(2,1)S(1)}, bf16[64,2048]{1,0:T(8,128)(2,1)S(1)}, u32[]{:S(2)}, u32[]{:S(2)}) collective-permute-start(bf16[64,2048]{1,0:T(8,128)(2,1)S(1)} %constant_dynamic-update-slice_fusion.2), channel_id=1, source_target_pairs={{0,224},{4,228},{8,232},{12,236},{16,240},{20,244},{24,248},{28,25... | collective-permute-start | bytes 786440 | tf_op jit(solution)/shard_map/ppermute | solution.py:394
  70.6 1.9 %copy-start = (f32[512,2048]{1,0:T(8,128)}, f32[512,2048]{1,0:T(8,128)S(1)}, u32[]{:S(2)}) copy-start(f32[512,2048]{1,0:T(8,128)S(1)} %get-tuple-element.39.acc_hbm) | copy-start | bytes 12582916
  72.5 1.4 copy-start.1
  73.9 6.1 %copy-start.2 = (bf16[2,128,1024]{2,1,0:T(8,128)(2,1)}, bf16[2,128,1024]{2,1,0:T(8,128)(2,1)S(1)}, u32[]{:S(2)}) copy-start(bf16[2,128,1024]{2,1,0:T(8,128)(2,1)S(1)} %collective-permute-done.9.m4) | copy-start | bytes 1572868
  74.0 6.0 %collective-permute-start.12 = (bf16[256,2048]{1,0:T(8,128)(2,1)S(1)}, bf16[256,2048]{1,0:T(8,128)(2,1)S(1)}, u32[]{:S(2)}, u32[]{:S(2)}) collective-permute-start(bf16[256,2048]{1,0:T(8,128)(2,1)S(1)} %constant_dynamic-update-slice_fusion.7.mine), channel_id=1, source_target_pairs={{0,4},{4,0},{8,12},{12,8},{16,20},{20,16},{24,28},{28,24},{32,36},... | collective-permute-start | bytes 3145736 | tf_op jit(solution)/shard_map/ppermute | solution.py:409
  77.9 2.1 %collective-permute-start.11 = (bf16[2,128,1024]{2,1,0:T(8,128)(2,1)}, bf16[2,128,1024]{2,1,0:T(8,128)(2,1)S(1)}, u32[]{:S(2)}, u32[]{:S(2)}) collective-permute-start(bf16[2,128,1024]{2,1,0:T(8,128)(2,1)} %broadcast_select_fusion), channel_id=1, source_target_pairs={{0,4},{4,0},{8,12},{12,8},{16,20},{20,16},{24,28},{28,24},{32,36},... | collective-permute-start | bytes 1572872 | tf_op jit(solution)/shard_map/ppermute | solution.py:410
  91.7 14.6 %collective-permute-start.15 = (bf16[512,512]{1,0:T(8,128)(2,1)S(1)}, bf16[512,512]{1,0:T(8,128)(2,1)S(1)}, u32[]{:S(2)}, u32[]{:S(2)}) collective-permute-start(bf16[512,512]{1,0:T(8,128)(2,1)S(1)} %get-tuple-element.46), channel_id=1, source_target_pairs={{0,3},{1,0},{2,1},{3,2},{4,7},{5,4},{6,5},{7,6},{8,11},{9,8},{10,9... | collective-permute-start | bytes 1572872 | tf_op jit(solution)/shard_map/ppermute | solution.py:413
  94.8 15.6 %collective-permute-start.13 = (bf16[512,512]{1,0:T(8,128)(2,1)S(1)}, bf16[512,512]{1,0:T(8,128)(2,1)S(1)}, u32[]{:S(2)}, u32[]{:S(2)}) collective-permute-start(bf16[512,512]{1,0:T(8,128)(2,1)S(1)} %get-tuple-element.44), channel_id=1, source_target_pairs={{0,1},{1,2},{2,3},{3,0},{4,5},{5,6},{6,7},{7,4},{8,9},{9,10},{10,1... | collective-permute-start | bytes 1572872 | tf_op jit(solution)/shard_map/ppermute | solution.py:413
  106.6 25.7 %collective-permute-start.16 = (bf16[512,1024]{1,0:T(8,128)(2,1)S(1)}, bf16[512,1024]{1,0:T(8,128)(2,1)S(1)}, u32[]{:S(2)}, u32[]{:S(2)}) collective-permute-start(bf16[512,1024]{1,0:T(8,128)(2,1)S(1)} %pad_maximum_fusion.1), channel_id=1, source_target_pairs={{0,3},{1,0},{2,1},{3,2},{4,7},{5,4},{6,5},{7,6},{8,11},{9,8},{10,9... | collective-permute-start | bytes 3145736 | tf_op jit(solution)/shard_map/ppermute | solution.py:413
  110.7 25.4 %collective-permute-start.14 = (bf16[512,1024]{1,0:T(8,128)(2,1)S(1)}, bf16[512,1024]{1,0:T(8,128)(2,1)S(1)}, u32[]{:S(2)}, u32[]{:S(2)}) collective-permute-start(bf16[512,1024]{1,0:T(8,128)(2,1)S(1)} %pad_maximum_fusion), channel_id=1, source_target_pairs={{0,1},{1,2},{2,3},{3,0},{4,5},{5,6},{6,7},{7,4},{8,9},{9,10},{10,1... | collective-permute-start | bytes 3145736 | tf_op jit(solution)/shard_map/ppermute | solution.py:413
where the time goes:
time: 140 us; the launch traced here: 138 us
  waiting for transfers between devices  61 us (44%)
  starting transfers between devices  34.5 us (25%)
  Pallas kernels  32.6 us (23%)
  local copies, waits for them, and re-layouts  5.2 us (4%)
  other arithmetic  4.14 us (3%)
    ppermute x4, waiting for transfers between devices, send(): lax.ppermute(block, 'head', [(i, (i + distance) % members) for i in range...  31.3 us
    ppermute x4, waiting for transfers between devices, shifted(): lax.ppermute(block, axis, [(i - distance, i) for i in devices if i - dist...  19.9 us
    ppermute x7, starting transfers between devices, move(): return lax.ppermute(block, 'seq', route)  15.5 us
    pallas_call x1, Pallas kernels, far(): pl.pallas_call(functools.partial(far_kernel, 256, heads, members, rows //...  11.7 us
    pallas_call x1, Pallas kernels, near(): pl.pallas_call(functools.partial(near_kernel, 256, heads), out_shape=(jax...  11.1 us
    ppermute x4, starting transfers between devices, shifted(): lax.ppermute(block, axis, [(i - distance, i) for i in devices if i - dist...  10.1 us
    ppermute x7, waiting for transfers between devices, move(): return lax.ppermute(block, 'seq', route)  7.7 us
    ppermute x4, starting transfers between devices, send(): lax.ppermute(block, 'head', [(i, (i + distance) % members) for i in range...  6.93 us
  transfers between devices with their start and end apart: 17, of which 8 were waited for; matrix products, arithmetic and copies ran while one was open for 2% of the time, Pallas kernels for 15%

commit v1 on v0

--- a/solution.py
+++ b/solution.py
@@ -140,8 +140,8 @@
 def near_kernel(
     tile, heads,
     pos_ref, q_hbm, k_hbm, v_hbm, ek_hbm, ev_hbm,
-    acc_ref, peak_ref,
-    q_ref, k_ref, v_ref, sems,
+    acc_hbm, peak_hbm,
+    q_ref, k_ref, v_ref, acc_ref, peak_ref, sems, out_sems,
 ):
     rows, n_edge = q_ref.shape[0], ek_hbm.shape[0]
     own, edge = pl.ds(n_edge, rows), pl.ds(0, n_edge)
@@ -157,6 +157,7 @@
         heads,
     )
     has_edge = pos_ref[0] >= 1
+    written = []
     on_diag = lax.broadcasted_iota(jnp.int32, (tile, tile), 1) <= lax.broadcasted_iota(
         jnp.int32, (tile, tile), 0
     )
@@ -177,6 +178,18 @@
                 s, peak, v_ref[: n + tile, c]
             )
             peak_ref[at, c] = jnp.broadcast_to(peak, (tile, HEAD_DIM))
+        c2 = pl.ds(2 * h * HEAD_DIM, 2 * HEAD_DIM)
+        written.append(
+            [
+                pltpu.make_async_copy(acc_ref.at[:, c2], acc_hbm.at[:, c2], out_sems.at[0, h]),
+                pltpu.make_async_copy(peak_ref.at[:, c], peak_hbm.at[:, c], out_sems.at[1, h]),
+            ]
+        )
+        for copy in written[h]:
+            copy.start()
+    for pair in written:
+        for copy in pair:
+            copy.wait()
 
 
 def near(position, queries, keys, values, edge_keys, edge_values):
@@ -185,19 +198,19 @@
     n_keys = edge_keys.shape[0] + rows
     return pl.pallas_call(
         functools.partial(near_kernel, 256, heads),
-        out_shape=(
-            jax.ShapeDtypeStruct((rows, 2 * width), F32),
-            jax.ShapeDtypeStruct((rows, width), F32),
-        ),
+        out_shape=(pltpu.HBM((rows, 2 * width), F32), pltpu.HBM((rows, width), F32)),
         in_specs=[SMEM] + [HBM] * 5,
-        out_specs=(VMEM, VMEM),
+        out_specs=(HBM, HBM),
         scratch_shapes=[
             pltpu.VMEM((rows, width), BF16),
             pltpu.VMEM((n_keys, width), BF16),
             pltpu.VMEM((n_keys, width), BF16),
+            pltpu.VMEM((rows, 2 * width), F32),
+            pltpu.VMEM((rows, width), F32),
             pltpu.SemaphoreType.DMA((5, heads)),
+            pltpu.SemaphoreType.DMA((2, heads)),
         ],
-        compiler_params=pltpu.CompilerParams(vmem_limit_bytes=24 << 20),
+        compiler_params=pltpu.CompilerParams(vmem_limit_bytes=32 << 20),
         cost_estimate=pl.CostEstimate(
             flops=rows * n_keys * width, bytes_accessed=1 << 20, transcendentals=0
         ),
@@ -207,7 +220,7 @@
 
 def far_kernel(
     tile, heads, members, per_coarse,
-    pos_ref, head_ref, q_hbm, m2, m3, m4, mine, other, acc_hbm, peak_hbm, w_hbm,
+    pos_ref, head_ref, q_hbm, m2, m3_even, m3_odd, m4, mine, other, acc_hbm, peak_hbm, w_hbm,
     att_ref, left_ref, right_ref,
     q_ref, k_ref, v_ref, acc_ref, peak_ref, w_ref, sems, w_sem,
 ):
@@ -226,10 +239,10 @@
             dst.at[pl.ds(to, size), pl.ds(g * 2 * HEAD_DIM, 2 * HEAD_DIM)],
         )
 
-    def group_copies(g):
+    def group_copies(g, m3):
         pairs = [whole(q_hbm, q_ref, g, 2 * HEAD_DIM)]
         to = 0
-        for m in (m2, m3, m4):
+        for m in (m3, m2, m4):
             pairs += [part(m.at[0], k_ref, g, to), part(m.at[1], v_ref, g, to)]
             to += n_med
         for c in (mine, other):
@@ -241,13 +254,28 @@
             pltpu.make_async_copy(src, dst, sems.at[t, g]) for t, (src, dst) in enumerate(pairs)
         ]
 
-    copies = [group_copies(g) for g in range(groups)]
+    copies = [group_copies(g, m3_even) for g in range(groups)]
+    even = pos_ref[0] % 2 == 0
+
+    def start(g):
+        @pl.when(even)
+        def _():
+            for copy in copies[g][1:3]:
+                copy.start()
+
+        @pl.when(jnp.logical_not(even))
+        def _():
+            for copy in group_copies(g, m3_odd)[1:3]:
+                copy.start()
+
+        for copy in copies[g][:1] + copies[g][3:]:
+            copy.start()
+
     block = lax.rem(head_ref[0] + 2, members)
     cols = pl.ds(pl.multiple_of(block * width, width), width)
     w_copy = pltpu.make_async_copy(w_hbm.at[:, cols], w_ref, w_sem.at[0])
     for g in range(2):
-        for copy in copies[g]:
-            copy.start()
+        start(g)
     w_copy.start()
     pos = pos_ref[0]
     j = lax.broadcasted_iota(jnp.int32, (1, n_coarse), 1) // per_coarse
@@ -257,7 +285,7 @@
     x = (pos % PLANE // 2 - j // 2 % CHIPS_X) & (CHIPS_X - 1)
     bias = [
         jnp.where(pos >= d, jnp.zeros((1, n_med), F32), jnp.full((1, n_med), NEG, F32))
-        for d in (2, 3, 4)
+        for d in (3, 2, 4)
     ]
     for core in (pos % 2, 1 - pos % 2):
         bias.append(jnp.where(z * PLANE + x * 2 + core < pos, 0.0, NEG))
@@ -267,8 +295,7 @@
             for copy in copies[h // 2]:
                 copy.wait()
             if h // 2 + 2 < groups:
-                for copy in copies[h // 2 + 2]:
-                    copy.start()
+                start(h // 2 + 2)
         c = head_cols(h)
         for i in range(rows // tile):
             at = pl.ds(i * tile, tile)
@@ -298,7 +325,7 @@
     return pl.pallas_call(
         functools.partial(far_kernel, 256, heads, members, rows // COARSE),
         out_shape=(jax.ShapeDtypeStruct((rows, width), BF16), half, half),
-        in_specs=[SMEM, SMEM] + [HBM] * 9,
+        in_specs=[SMEM, SMEM] + [HBM] * 10,
         out_specs=(VMEM, VMEM, VMEM),
         scratch_shapes=[
             pltpu.VMEM((rows, width), BF16),
@@ -320,8 +347,8 @@
         head,
         in_hbm(queries),
         in_hbm(meds[0]),
-        meds[1],
-        in_hbm(meds[2]),
+        *meds[1:3],
+        in_hbm(meds[3]),
         *coarse,
         in_hbm(acc),
         in_hbm(peak),
@@ -378,7 +405,6 @@
     position = lax.axis_index("seq")
     pos = position.astype(jnp.int32).reshape(1)
     head = lax.axis_index("head").astype(jnp.int32).reshape(1)
-    core0 = (position & 1) == 0
     swap = [(i, i ^ 1) for i in range(n_seq)]
 
     def place(z, x, core):
@@ -401,13 +427,23 @@
     edge_keys, values, ring, med = lax.optimization_barrier((edge_keys, values, ring, med))
     edge_values = shifted(values, "seq", 1)
     rings = [move(ring, d, 0) for d in (-1, -2, 1)]
+    turned = move(med, 0, -1)
+    rings, edge_values, turned, med = lax.optimization_barrier((rings, edge_values, turned, med))
     med2 = shifted(med, "seq", 2)
-    med4 = shifted(med, "seq", 4)
+    last = [
+        (place(z, x, c), place(z + (x + 1) % CHIPS_X // 2, (x - 1) % CHIPS_X, c))
+        for z in range(PLANES)
+        for x in range(CHIPS_X)
+        for c in range(2)
+        if z + (x + 1) % CHIPS_X // 2 < PLANES
+    ]
+    med4 = lax.ppermute(turned, "seq", last)
     acc, peak = near(pos, queries, keys, values, edge_keys, edge_values)
-    rings, med2, med4, acc, peak = lax.optimization_barrier((rings, med2, med4, acc, peak))
+    med2, med4, acc, peak = lax.optimization_barrier((med2, med4, acc, peak))
     mine = jnp.concatenate([ring] + rings, 0)
     other = lax.ppermute(mine, "seq", swap)
-    med3 = lax.ppermute(jnp.where(core0, med2, med4), "seq", swap)
+    med3_even = lax.ppermute(med4, "seq", [(i + 1, i) for i in range(0, n_seq, 2)])
+    med3_odd = lax.ppermute(med2, "seq", [(i, i + 1) for i in range(0, n_seq, 2)])
 
     def send(block, distance):
         return lax.ppermute(
@@ -415,7 +451,7 @@
         )
 
     attention, left, right = far(
-        pos, head, queries, (med2, med3, med4), (mine, other), acc, peak, out_weight
+        pos, head, queries, (med2, med3_even, med3_odd, med4), (mine, other), acc, peak, out_weight
     )
     left, right = send(left, 1), send(right, -1)
     ahead, behind, own = project(head, attention, out_weight, members, (1, members - 1, 0))

time: 140 us -> 141 us (level)
  starting transfers between devices: 34.5 us -> 39.2 us
  local copies, waits for them, and re-layouts: 5.2 us -> 1.91 us
  Pallas kernels: 32.6 us -> 34.7 us
  other arithmetic: 4.14 us -> 2.25 us
    ppermute x4 -> x3, waiting for transfers between devices: 19.9 us -> 0.01 us  [shifted(): lax.ppermute(block, axis, [(i - distance, i) for i in devices if i - dist...]
    ppermute x7 -> x8, waiting for transfers between devices: 7.7 us -> 26.3 us  [move(): return lax.ppermute(block, 'seq', route)]
    ppermute x1 -> x3, starting transfers between devices: 0.01 us -> 9.77 us  [the longest x1 6.06 us: body(): med4 = lax.ppermute(turned, 'seq', last)]
    ppermute x4 -> x3, starting transfers between devices: 10.1 us -> 6.06 us  [shifted(): lax.ppermute(block, axis, [(i - distance, i) for i in devices if i - dist...]
    unnamed x15 -> x11, local copies, waits for them, and re-layouts: 5.1 us -> 1.81 us
    select_n x1 -> x0, other arithmetic: 1.89 us -> none  [body(): med3 = lax.ppermute(jnp.where(core0, med2, med4), 'seq', swap)]
    ppermute x1, starting transfers between devices: 2 us -> 0.27 us  [body(): other = lax.ppermute(mine, 'seq', swap)]
    ppermute x7 -> x8, starting transfers between devices: 15.5 us -> 16.2 us  [move(): return lax.ppermute(block, 'seq', route)]
  transfers between devices with their start and end apart: 17 -> 19, of which waited for: 8 -> 11; matrix products, arithmetic and copies ran while one was open for 2% -> 1% of each run, Pallas kernels for 15% -> 16%
where the time goes in v1:
time: 141 us; the launch traced here: 139 us
  waiting for transfers between devices  60.3 us (43%)
  starting transfers between devices  39.2 us (28%)
  Pallas kernels  34.7 us (25%)
  other arithmetic  2.25 us (2%)
  local copies, waits for them, and re-layouts  1.91 us (1%)
    ppermute x4, waiting for transfers between devices, send(): lax.ppermute(block, 'head', [(i, (i + distance) % members) for i in range...  31.2 us
    ppermute x8, waiting for transfers between devices, move(): return lax.ppermute(block, 'seq', route)  26.3 us
    ppermute x8, starting transfers between devices, move(): return lax.ppermute(block, 'seq', route)  16.2 us
    pallas_call x1, Pallas kernels, near(): pl.pallas_call(functools.partial(near_kernel, 256, heads), out_shape=(plt...  12.1 us
    pallas_call x1, Pallas kernels, far(): pl.pallas_call(functools.partial(far_kernel, 256, heads, members, rows //...  11.9 us
    ppermute x4, starting transfers between devices, send(): lax.ppermute(block, 'head', [(i, (i + distance) % members) for i in range...  6.94 us
    ppermute x3, starting transfers between devices, shifted(): lax.ppermute(block, axis, [(i - distance, i) for i in devices if i - dist...  6.06 us
    ppermute x1, starting transfers between devices, body(): med4 = lax.ppermute(turned, 'seq', last)  6.06 us
  transfers between devices with their start and end apart: 19, of which 11 were waited for; matrix products, arithmetic and copies ran while one was open for 1% of the time, Pallas kernels for 16%

profile of v1, /device:TPU:96, one launch (start us, length us, event | category | flops | bytes accessed | tf_op | source)
XLA Modules:
  0.0 138.6 jit_solution(16936636629143869264)
XLA Ops:
  0.0 2.0 %collective-permute-start = (bf16[512,1024]{1,0:T(8,128)(2,1)}, bf16[512,1024]{1,0:T(8,128)(2,1)S(1)}, u32[]{:S(2)}, u32[]{:S(2)}) collective-permute-start(bf16[512,1024]{1,0:T(8,128)(2,1)} %k_hbm.3), channel_id=1, source_target_pairs={{0,4},{4,8},{8,12},{12,16},{16,20},{20,24},{24,28},{28,32},{32,36}... | collective-permute-start | bytes 3145736 | tf_op jit(solution)/shard_map/ppermute | solution.py:397
  2.8 5.3 %pool.1 = (bf16[2,128,1024]{2,1,0:T(8,128)(2,1)}, bf16[8,2048]{1,0:T(8,128)(2,1)S(1)}) custom-call(bf16[512,1024]{1,0:T(8,128)(2,1)} %k_hbm.3, bf16[512,1024]{1,0:T(8,128)(2,1)} %v_hbm.2, f32[2,8,4]{2,1,0:T(8,128)S(1)} %copy.7.mw_ref, f32[2,8,64]{2,1,0:T(8,128)} %cw_hbm.1), custom_call_target="tpu_custom_call" | custom-call | flops 570425344 | bytes 3145728 | tf_op jit(solution)/shard_map/pool/pallas_call | solution.py:107
  8.1 4.6 %collective-permute-start.1 = (bf16[8,2048]{1,0:T(8,128)(2,1)S(1)}, bf16[8,2048]{1,0:T(8,128)(2,1)S(1)}, u32[]{:S(2)}, u32[]{:S(2)}) collective-permute-start(bf16[8,2048]{1,0:T(8,128)(2,1)S(1)} %get-tuple-element.29), channel_id=1, source_target_pairs={{0,128},{4,132},{8,136},{12,140},{16,144},{20,148},{24,152},{28,15... | collective-permute-start | bytes 98312 | tf_op jit(solution)/shard_map/ppermute | solution.py:420
  12.7 3.3 %collective-permute-done.1 = bf16[8,2048]{1,0:T(8,128)(2,1)S(1)} collective-permute-done((bf16[8,2048]{1,0:T(8,128)(2,1)S(1)}, bf16[8,2048]{1,0:T(8,128)(2,1)S(1)}, u32[]{:S(2)}, u32[]{:S(2)}) %collective-permute-start.1) | collective-permute-done | bytes 32800 | tf_op jit(solution)/shard_map/ppermute | solution.py:420
  19.3 1.8 %collective-permute-start.3 = (bf16[16,2048]{1,0:T(8,128)(2,1)S(1)}, bf16[16,2048]{1,0:T(8,128)(2,1)S(1)}, u32[]{:S(2)}, u32[]{:S(2)}) collective-permute-start(bf16[16,2048]{1,0:T(8,128)(2,1)S(1)} %get-tuple-element.53), channel_id=1, source_target_pairs={{0,16},{4,20},{8,24},{12,28},{16,0},{20,4},{24,8},{28,12},{32,48},... | collective-permute-start | bytes 196616 | tf_op jit(solution)/shard_map/ppermute | solution.py:420
  21.5 4.0 %collective-permute-done.3 = bf16[16,2048]{1,0:T(8,128)(2,1)S(1)} collective-permute-done((bf16[16,2048]{1,0:T(8,128)(2,1)S(1)}, bf16[16,2048]{1,0:T(8,128)(2,1)S(1)}, u32[]{:S(2)}, u32[]{:S(2)}) %collective-permute-start.3) | collective-permute-done | bytes 65568 | tf_op jit(solution)/shard_map/ppermute | solution.py:420
  26.5 2.0 %collective-permute-start.8 = (bf16[512,1024]{1,0:T(8,128)(2,1)S(1)}, bf16[512,1024]{1,0:T(8,128)(2,1)S(1)}, u32[]{:S(2)}, u32[]{:S(2)}) collective-permute-start(bf16[512,1024]{1,0:T(8,128)(2,1)S(1)} %copy-done), channel_id=1, source_target_pairs={{0,4},{4,8},{8,12},{12,16},{16,20},{20,24},{24,28},{28,32},{32,36}... | collective-permute-start | bytes 3145736 | tf_op jit(solution)/shard_map/ppermute | solution.py:397
  30.1 3.1 %collective-permute-start.7 = (bf16[64,2048]{1,0:T(8,128)(2,1)S(1)}, bf16[64,2048]{1,0:T(8,128)(2,1)S(1)}, u32[]{:S(2)}, u32[]{:S(2)}) collective-permute-start(bf16[64,2048]{1,0:T(8,128)(2,1)S(1)} %constant_dynamic-update-slice_fusion.2), channel_id=1, source_target_pairs={{0,32},{4,36},{8,40},{12,44},{16,48},{20,52},{24,56},{28,60},{32,6... | collective-permute-start | bytes 786440 | tf_op jit(solution)/shard_map/ppermute | solution.py:420
  33.2 1.9 %collective-permute-start.6 = (bf16[64,2048]{1,0:T(8,128)(2,1)S(1)}, bf16[64,2048]{1,0:T(8,128)(2,1)S(1)}, u32[]{:S(2)}, u32[]{:S(2)}) collective-permute-start(bf16[64,2048]{1,0:T(8,128)(2,1)S(1)} %constant_dynamic-update-slice_fusion.2), channel_id=1, source_target_pairs={{0,192},{4,196},{8,200},{12,204},{16,208},{20,212},{24,216},{28,22... | collective-permute-start | bytes 786440 | tf_op jit(solution)/shard_map/ppermute | solution.py:420
  35.1 4.4 %collective-permute-done.7 = bf16[64,2048]{1,0:T(8,128)(2,1)S(1)} collective-permute-done((bf16[64,2048]{1,0:T(8,128)(2,1)S(1)}, bf16[64,2048]{1,0:T(8,128)(2,1)S(1)}, u32[]{:S(2)}, u32[]{:S(2)}) %collective-permute-start.7) | collective-permute-done | bytes 262176 | tf_op jit(solution)/shard_map/ppermute | solution.py:420
  39.4 9.0 %collective-permute-done.6 = bf16[64,2048]{1,0:T(8,128)(2,1)S(1)} collective-permute-done((bf16[64,2048]{1,0:T(8,128)(2,1)S(1)}, bf16[64,2048]{1,0:T(8,128)(2,1)S(1)}, u32[]{:S(2)}, u32[]{:S(2)}) %collective-permute-start.6) | collective-permute-done | bytes 262176 | tf_op jit(solution)/shard_map/ppermute | solution.py:420
  48.4 5.2 %collective-permute-done.5 = bf16[64,2048]{1,0:T(8,128)(2,1)S(1)} collective-permute-done((bf16[64,2048]{1,0:T(8,128)(2,1)S(1)}, bf16[64,2048]{1,0:T(8,128)(2,1)S(1)}, u32[]{:S(2)}, u32[]{:S(2)}) %collective-permute-start.5) | collective-permute-done | bytes 262176 | tf_op jit(solution)/shard_map/ppermute | solution.py:420
  53.7 2.0 %collective-permute-start.10 = (bf16[2,128,1024]{2,1,0:T(8,128)(2,1)}, bf16[2,128,1024]{2,1,0:T(8,128)(2,1)}, u32[]{:S(2)}, u32[]{:S(2)}) collective-permute-start(bf16[2,128,1024]{2,1,0:T(8,128)(2,1)} %get-tuple-element.34), channel_id=1, source_target_pairs={{0,8},{4,12},{8,16},{12,20},{16,24},{20,28},{24,32},{28,36},{32,40... | collective-permute-start | bytes 1572872 | tf_op jit(solution)/shard_map/ppermute | solution.py:397
  55.7 6.1 %collective-permute-start.11 = (bf16[2,128,1024]{2,1,0:T(8,128)(2,1)}, bf16[2,128,1024]{2,1,0:T(8,128)(2,1)}, u32[]{:S(2)}, u32[]{:S(2)}) collective-permute-start(bf16[2,128,1024]{2,1,0:T(8,128)(2,1)} %collective-permute-done.9), channel_id=1, source_target_pairs={{0,24},{4,28},{8,32},{12,36},{16,40},{20,44},{24,16},{28,20},{32,5... | collective-permute-start | bytes 1572872 | tf_op jit(solution)/shard_map/ppermute | solution.py:440
  62.1 12.1 %near.1 = (f32[512,2048]{1,0:T(8,128)}, f32[512,1024]{1,0:T(8,128)}) custom-call(s32[1]{0:T(128)} %bitcast.1.pos_ref, bf16[512,1024]{1,0:T(8,128)(2,1)} %q_hbm.3, bf16[512,1024]{1,0:T(8,128)(2,1)} %k_hbm.3, bf16[512,1024]{1,0:T(8,128)(2,1)} %v_hbm.2, bf16[512,1024]{1,0:T(8,128)(2,1)} %copy-done.1, bf16[512,1024]{1,0:T(8,128)(2,1)S(1)} %collective-permute-done.8.ev_hbm), custom_call_target="tpu_custom_call" | custom-call | flops 536870912 | bytes 1048576 | tf_op jit(solution)/shard_map/near/pallas_call | solution.py:199
  74.2 2.4 %collective-permute-start.13 = (bf16[2,128,1024]{2,1,0:T(8,128)(2,1)}, bf16[2,128,1024]{2,1,0:T(8,128)(2,1)S(1)}, u32[]{:S(2)}, u32[]{:S(2)}) collective-permute-start(bf16[2,128,1024]{2,1,0:T(8,128)(2,1)} %collective-permute-done.10.m2), channel_id=1, source_target_pairs={{0,4},{8,12},{16,20},{24,28},{32,36},{40,44},{48,52},{56,60},{64,6... | collective-permute-start | bytes 1572872 | tf_op jit(solution)/shard_map/ppermute | solution.py:446
  78.4 2.3 %collective-permute-done.12.m3_even = bf16[2,128,1024]{2,1,0:T(8,128)(2,1)S(1)} collective-permute-done((bf16[2,128,1024]{2,1,0:T(8,128)(2,1)}, bf16[2,128,1024]{2,1,0:T(8,128)(2,1)S(1)}, u32[]{:S(2)}, u32[]{:S(2)}) %collective-permute-start.12) | collective-permute-done | bytes 524320 | tf_op jit(solution)/shard_map/ppermute | solution.py:445
  80.7 11.9 %far.1 = (bf16[512,1024]{1,0:T(8,128)(2,1)S(1)}, bf16[512,512]{1,0:T(8,128)(2,1)S(1)}, bf16[512,512]{1,0:T(8,128)(2,1)S(1)}) custom-call(s32[1]{0:T(128)} %bitcast.1.pos_ref, s32[1]{0:T(128)} %bitcast.head_ref, bf16[512,1024]{1,0:T(8,128)(2,1)} %q_hbm.3, bf16[2,128,1024]{2,1,0:T(8,128)(2,1)} %collective-permute-done.10.m2, ...), custom_call_target="tpu_custom_call" | custom-call | flops 3758096384 | bytes 2097152 | tf_op jit(solution)/shard_map/far/pallas_call | solution.py:325
  92.6 3.1 %collective-permute-start.17 = (bf16[512,512]{1,0:T(8,128)(2,1)S(1)}, bf16[512,512]{1,0:T(8,128)(2,1)S(1)}, u32[]{:S(2)}, u32[]{:S(2)}) collective-permute-start(bf16[512,512]{1,0:T(8,128)(2,1)S(1)} %get-tuple-element.52), channel_id=1, source_target_pairs={{0,3},{1,0},{2,1},{3,2},{4,7},{5,4},{6,5},{7,6},{8,11},{9,8},{10,9... | collective-permute-start | bytes 1572872 | tf_op jit(solution)/shard_map/ppermute | solution.py:449
  95.7 5.4 %project.1 = (bf16[512,1024]{1,0:T(8,128)(2,1)S(1)}, bf16[512,1024]{1,0:T(8,128)(2,1)S(1)}, bf16[512,1024]{1,0:T(8,128)(2,1)S(1)}) custom-call(s32[1]{0:T(128)} %bitcast.head_ref, bf16[512,1024]{1,0:T(8,128)(2,1)S(1)} %get-tuple-element.47.a_ref, bf16[1024,4096]{1,0:T(8,128)(2,1)} %w_hbm.3), custom_call_target="tpu_custom_call" | custom-call | flops 3221225472 | bytes 6291456 | tf_op jit(solution)/shard_map/project/pallas_call | solution.py:376
  101.2 6.0 %collective-permute-done.17 = bf16[512,512]{1,0:T(8,128)(2,1)S(1)} collective-permute-done((bf16[512,512]{1,0:T(8,128)(2,1)S(1)}, bf16[512,512]{1,0:T(8,128)(2,1)S(1)}, u32[]{:S(2)}, u32[]{:S(2)}) %collective-permute-start.17) | collective-permute-done | bytes 524320 | tf_op jit(solution)/shard_map/ppermute | solution.py:449
  107.5 3.8 %collective-permute-start.18 = (bf16[512,1024]{1,0:T(8,128)(2,1)S(1)}, bf16[512,1024]{1,0:T(8,128)(2,1)S(1)}, u32[]{:S(2)}, u32[]{:S(2)}) collective-permute-start(bf16[512,1024]{1,0:T(8,128)(2,1)S(1)} %pad_maximum_fusion.1), channel_id=1, source_target_pairs={{0,3},{1,0},{2,1},{3,2},{4,7},{5,4},{6,5},{7,6},{8,11},{9,8},{10,9... | collective-permute-start | bytes 3145736 | tf_op jit(solution)/shard_map/ppermute | solution.py:449
  111.7 21.4 %collective-permute-done.18 = bf16[512,1024]{1,0:T(8,128)(2,1)S(1)} collective-permute-done((bf16[512,1024]{1,0:T(8,128)(2,1)S(1)}, bf16[512,1024]{1,0:T(8,128)(2,1)S(1)}, u32[]{:S(2)}, u32[]{:S(2)}) %collective-permute-start.18) | collective-permute-done | bytes 1048608 | tf_op jit(solution)/shard_map/ppermute | solution.py:449
  133.2 3.8 %collective-permute-done.16 = bf16[512,1024]{1,0:T(8,128)(2,1)S(1)} collective-permute-done((bf16[512,1024]{1,0:T(8,128)(2,1)S(1)}, bf16[512,1024]{1,0:T(8,128)(2,1)S(1)}, u32[]{:S(2)}, u32[]{:S(2)}) %collective-permute-start.16) | collective-permute-done | bytes 1048608 | tf_op jit(solution)/shard_map/ppermute | solution.py:449
  (39 shorter events, 11.5 us)
Async XLA Ops:
  0.0 26.5 %copy-start = (bf16[512,1024]{1,0:T(8,128)(2,1)S(1)}, bf16[512,1024]{1,0:T(8,128)(2,1)}, u32[]{:S(2)}) copy-start(bf16[512,1024]{1,0:T(8,128)(2,1)} %v_hbm.2) | copy-start | bytes 3145732
  0.0 25.5 %collective-permute-start = (bf16[512,1024]{1,0:T(8,128)(2,1)}, bf16[512,1024]{1,0:T(8,128)(2,1)S(1)}, u32[]{:S(2)}, u32[]{:S(2)}) collective-permute-start(bf16[512,1024]{1,0:T(8,128)(2,1)} %k_hbm.3), channel_id=1, source_target_pairs={{0,4},{4,8},{8,12},{12,16},{16,20},{20,24},{24,28},{28,32},{32,36}... | collective-permute-start | bytes 3145736 | tf_op jit(solution)/shard_map/ppermute | solution.py:397
  8.1 7.9 %collective-permute-start.1 = (bf16[8,2048]{1,0:T(8,128)(2,1)S(1)}, bf16[8,2048]{1,0:T(8,128)(2,1)S(1)}, u32[]{:S(2)}, u32[]{:S(2)}) collective-permute-start(bf16[8,2048]{1,0:T(8,128)(2,1)S(1)} %get-tuple-element.29), channel_id=1, source_target_pairs={{0,128},{4,132},{8,136},{12,140},{16,144},{20,148},{24,152},{28,15... | collective-permute-start | bytes 98312 | tf_op jit(solution)/shard_map/ppermute | solution.py:420
  16.0 5.5 %collective-permute-start.2 = (bf16[16,2048]{1,0:T(8,128)(2,1)S(1)}, bf16[16,2048]{1,0:T(8,128)(2,1)S(1)}, u32[]{:S(2)}, u32[]{:S(2)}) collective-permute-start(bf16[16,2048]{1,0:T(8,128)(2,1)S(1)} %get-tuple-element.53), channel_id=1, source_target_pairs={{0,8},{4,12},{8,16},{12,20},{16,24},{20,28},{24,0},{28,4},{32,40},... | collective-permute-start | bytes 196616 | tf_op jit(solution)/shard_map/ppermute | solution.py:420
  17.5 8.0 %collective-permute-start.4 = (bf16[16,2048]{1,0:T(8,128)(2,1)S(1)}, bf16[16,2048]{1,0:T(8,128)(2,1)S(1)}, u32[]{:S(2)}, u32[]{:S(2)}) collective-permute-start(bf16[16,2048]{1,0:T(8,128)(2,1)S(1)} %get-tuple-element.53), channel_id=1, source_target_pairs={{0,24},{4,28},{8,0},{12,4},{16,8},{20,12},{24,16},{28,20},{32,56},... | collective-permute-start | bytes 196616 | tf_op jit(solution)/shard_map/ppermute | solution.py:420
  19.3 6.2 %collective-permute-start.3 = (bf16[16,2048]{1,0:T(8,128)(2,1)S(1)}, bf16[16,2048]{1,0:T(8,128)(2,1)S(1)}, u32[]{:S(2)}, u32[]{:S(2)}) collective-permute-start(bf16[16,2048]{1,0:T(8,128)(2,1)S(1)} %get-tuple-element.53), channel_id=1, source_target_pairs={{0,16},{4,20},{8,24},{12,28},{16,0},{20,4},{24,8},{28,12},{32,48},... | collective-permute-start | bytes 196616 | tf_op jit(solution)/shard_map/ppermute | solution.py:420
  25.5 1.0 copy-start.1
  26.5 27.2 %collective-permute-start.8 = (bf16[512,1024]{1,0:T(8,128)(2,1)S(1)}, bf16[512,1024]{1,0:T(8,128)(2,1)S(1)}, u32[]{:S(2)}, u32[]{:S(2)}) collective-permute-start(bf16[512,1024]{1,0:T(8,128)(2,1)S(1)} %copy-done), channel_id=1, source_target_pairs={{0,4},{4,8},{8,12},{12,16},{16,20},{20,24},{24,28},{28,32},{32,36}... | collective-permute-start | bytes 3145736 | tf_op jit(solution)/shard_map/ppermute | solution.py:397
  28.5 25.2 %collective-permute-start.9 = (bf16[2,128,1024]{2,1,0:T(8,128)(2,1)}, bf16[2,128,1024]{2,1,0:T(8,128)(2,1)}, u32[]{:S(2)}, u32[]{:S(2)}) collective-permute-start(bf16[2,128,1024]{2,1,0:T(8,128)(2,1)} %get-tuple-element.34), channel_id=1, source_target_pairs={{0,24},{4,28},{8,0},{12,4},{16,8},{20,12},{24,16},{28,20},{32,56},... | collective-permute-start | bytes 1572872 | tf_op jit(solution)/shard_map/ppermute | solution.py:420
  30.1 9.4 %collective-permute-start.7 = (bf16[64,2048]{1,0:T(8,128)(2,1)S(1)}, bf16[64,2048]{1,0:T(8,128)(2,1)S(1)}, u32[]{:S(2)}, u32[]{:S(2)}) collective-permute-start(bf16[64,2048]{1,0:T(8,128)(2,1)S(1)} %constant_dynamic-update-slice_fusion.2), channel_id=1, source_target_pairs={{0,32},{4,36},{8,40},{12,44},{16,48},{20,52},{24,56},{28,60},{32,6... | collective-permute-start | bytes 786440 | tf_op jit(solution)/shard_map/ppermute | solution.py:420
  33.2 15.3 %collective-permute-start.6 = (bf16[64,2048]{1,0:T(8,128)(2,1)S(1)}, bf16[64,2048]{1,0:T(8,128)(2,1)S(1)}, u32[]{:S(2)}, u32[]{:S(2)}) collective-permute-start(bf16[64,2048]{1,0:T(8,128)(2,1)S(1)} %constant_dynamic-update-slice_fusion.2), channel_id=1, source_target_pairs={{0,192},{4,196},{8,200},{12,204},{16,208},{20,212},{24,216},{28,22... | collective-permute-start | bytes 786440 | tf_op jit(solution)/shard_map/ppermute | solution.py:420
  35.0 18.6 %collective-permute-start.5 = (bf16[64,2048]{1,0:T(8,128)(2,1)S(1)}, bf16[64,2048]{1,0:T(8,128)(2,1)S(1)}, u32[]{:S(2)}, u32[]{:S(2)}) collective-permute-start(bf16[64,2048]{1,0:T(8,128)(2,1)S(1)} %constant_dynamic-update-slice_fusion.2), channel_id=1, source_target_pairs={{0,224},{4,228},{8,232},{12,236},{16,240},{20,244},{24,248},{28,25... | collective-permute-start | bytes 786440 | tf_op jit(solution)/shard_map/ppermute | solution.py:420
  53.7 20.5 %collective-permute-start.10 = (bf16[2,128,1024]{2,1,0:T(8,128)(2,1)}, bf16[2,128,1024]{2,1,0:T(8,128)(2,1)}, u32[]{:S(2)}, u32[]{:S(2)}) collective-permute-start(bf16[2,128,1024]{2,1,0:T(8,128)(2,1)} %get-tuple-element.34), channel_id=1, source_target_pairs={{0,8},{4,12},{8,16},{12,20},{16,24},{20,28},{24,32},{28,36},{32,40... | collective-permute-start | bytes 1572872 | tf_op jit(solution)/shard_map/ppermute | solution.py:397
  55.7 18.5 %collective-permute-start.11 = (bf16[2,128,1024]{2,1,0:T(8,128)(2,1)}, bf16[2,128,1024]{2,1,0:T(8,128)(2,1)}, u32[]{:S(2)}, u32[]{:S(2)}) collective-permute-start(bf16[2,128,1024]{2,1,0:T(8,128)(2,1)} %collective-permute-done.9), channel_id=1, source_target_pairs={{0,24},{4,28},{8,32},{12,36},{16,40},{20,44},{24,16},{28,20},{32,5... | collective-permute-start | bytes 1572872 | tf_op jit(solution)/shard_map/ppermute | solution.py:440
  61.8 16.1 %collective-permute-start.14 = (bf16[256,2048]{1,0:T(8,128)(2,1)S(1)}, bf16[256,2048]{1,0:T(8,128)(2,1)S(1)}, u32[]{:S(2)}, u32[]{:S(2)}) collective-permute-start(bf16[256,2048]{1,0:T(8,128)(2,1)S(1)} %constant_dynamic-update-slice_fusion.7.mine), channel_id=1, source_target_pairs={{0,4},{4,0},{8,12},{12,8},{16,20},{20,16},{24,28},{28,24},{32,36},... | collective-permute-start | bytes 3145736 | tf_op jit(solution)/shard_map/ppermute | solution.py:444
  74.2 4.1 %collective-permute-start.13 = (bf16[2,128,1024]{2,1,0:T(8,128)(2,1)}, bf16[2,128,1024]{2,1,0:T(8,128)(2,1)S(1)}, u32[]{:S(2)}, u32[]{:S(2)}) collective-permute-start(bf16[2,128,1024]{2,1,0:T(8,128)(2,1)} %collective-permute-done.10.m2), channel_id=1, source_target_pairs={{0,4},{8,12},{16,20},{24,28},{32,36},{40,44},{48,52},{56,60},{64,6... | collective-permute-start | bytes 1572872 | tf_op jit(solution)/shard_map/ppermute | solution.py:446
  76.7 4.0 %collective-permute-start.12 = (bf16[2,128,1024]{2,1,0:T(8,128)(2,1)}, bf16[2,128,1024]{2,1,0:T(8,128)(2,1)S(1)}, u32[]{:S(2)}, u32[]{:S(2)}) collective-permute-start(bf16[2,128,1024]{2,1,0:T(8,128)(2,1)} %collective-permute-done.11.m4), channel_id=1, source_target_pairs={{4,0},{12,8},{20,16},{28,24},{36,32},{44,40},{52,48},{60,56},{68,6... | collective-permute-start | bytes 1572872 | tf_op jit(solution)/shard_map/ppermute | solution.py:445
  92.6 14.6 %collective-permute-start.17 = (bf16[512,512]{1,0:T(8,128)(2,1)S(1)}, bf16[512,512]{1,0:T(8,128)(2,1)S(1)}, u32[]{:S(2)}, u32[]{:S(2)}) collective-permute-start(bf16[512,512]{1,0:T(8,128)(2,1)S(1)} %get-tuple-element.52), channel_id=1, source_target_pairs={{0,3},{1,0},{2,1},{3,2},{4,7},{5,4},{6,5},{7,6},{8,11},{9,8},{10,9... | collective-permute-start | bytes 1572872 | tf_op jit(solution)/shard_map/ppermute | solution.py:449
  95.7 15.6 %collective-permute-start.15 = (bf16[512,512]{1,0:T(8,128)(2,1)S(1)}, bf16[512,512]{1,0:T(8,128)(2,1)S(1)}, u32[]{:S(2)}, u32[]{:S(2)}) collective-permute-start(bf16[512,512]{1,0:T(8,128)(2,1)S(1)} %get-tuple-element.50), channel_id=1, source_target_pairs={{0,1},{1,2},{2,3},{3,0},{4,5},{5,6},{6,7},{7,4},{8,9},{9,10},{10,1... | collective-permute-start | bytes 1572872 | tf_op jit(solution)/shard_map/ppermute | solution.py:449
  107.5 25.6 %collective-permute-start.18 = (bf16[512,1024]{1,0:T(8,128)(2,1)S(1)}, bf16[512,1024]{1,0:T(8,128)(2,1)S(1)}, u32[]{:S(2)}, u32[]{:S(2)}) collective-permute-start(bf16[512,1024]{1,0:T(8,128)(2,1)S(1)} %pad_maximum_fusion.1), channel_id=1, source_target_pairs={{0,3},{1,0},{2,1},{3,2},{4,7},{5,4},{6,5},{7,6},{8,11},{9,8},{10,9... | collective-permute-start | bytes 3145736 | tf_op jit(solution)/shard_map/ppermute | solution.py:449
  111.6 25.4 %collective-permute-start.16 = (bf16[512,1024]{1,0:T(8,128)(2,1)S(1)}, bf16[512,1024]{1,0:T(8,128)(2,1)S(1)}, u32[]{:S(2)}, u32[]{:S(2)}) collective-permute-start(bf16[512,1024]{1,0:T(8,128)(2,1)S(1)} %pad_maximum_fusion), channel_id=1, source_target_pairs={{0,1},{1,2},{2,3},{3,0},{4,5},{5,6},{6,7},{7,4},{8,9},{9,10},{10,1... | collective-permute-start | bytes 3145736 | tf_op jit(solution)/shard_map/ppermute | solution.py:449
